TPU v7x, 32 devices: a whole 2x2x4 slice. The times are simulated.
32 devices in a mesh: groups: 2 (over y), seq: 4 (over z), head: 2 (over x), sub: 2 (over core).
Axes of the slice: x: 2, y: 2, z: 4, core: 2. Of those that a mesh axis runs over, the one named last changes fastest.
Arguments:
- hidden_states: bfloat16 [8192, 8192], P(('groups', 'seq', 'sub'), 'head'), parts along dimension 0, may hold values from -42 to 42
- key_projection_weight: bfloat16 [8192, 1024], P(('seq', 'sub'), 'head'), may hold values from -0.0625 to 0.0625
- value_projection_weight: bfloat16 [8192, 1024], P(('seq', 'sub'), 'head'), may hold values from -0.0625 to 0.0625
- head_basis_matrix: float32 [8, 128, 64], P('head'), may hold values from -0.5 to 0.5
- slot_token: int32 [8192], P(('groups', 'seq', 'sub')), parts along dimension 0, may hold values from 0 to 4095, as said below
Outputs:
- compressed_keys: bfloat16 [8192, 512], P(('groups', 'seq', 'sub'), 'head'), parts along dimension 0
- value_cache: bfloat16 [8192, 1024], P(('groups', 'seq', 'sub'), 'head'), parts along dimension 0
There are 2 independent parts, one for each index of `groups`. A program takes and returns all parts, laid end to end along the dimension named above; an argument that names none is the same for every part. Nothing has to cross between parts.
Inputs may be any that keep to these rules, and one draw needn't show every extreme that they name: `slot_token`: A permutation of the 4096 token positions. Each aligned block of 512 rows holds exactly 64 positions of each aligned block of 512 positions.
All inputs are finite; a program needn't handle non-finite values.
Results may differ from a plain program's by a relative error of at most 0.0055.
Values may be sent and summed in bfloat16 or wider, within the bound.
No kernel may reach another device: no remote copies, remote signals or barrier semaphores. Data moves between devices by JAX's collectives and lax.ppermute only.
A program may use at most 64 MiB of HBM per device.

v0:
```python
import jax
import jax.numpy as jnp
from jax import lax
from jax.sharding import PartitionSpec as P

ridge_share = 0.05


def covariance_sum(decode_key_cache, heads_here, head_dim, token_total):
    per_head_keys = decode_key_cache.reshape(decode_key_cache.shape[0], heads_here, head_dim)
    local_terms = jnp.einsum(
        "thi,thj->hij", per_head_keys, per_head_keys, preferred_element_type=jnp.float32
    )
    summed = lax.psum(local_terms, ("seq", "sub"))
    return summed / token_total


def per_device(
    hidden_states, key_projection_weight, value_projection_weight, head_basis_matrix, slot_token
):
    tokens_here = hidden_states.shape[0]
    seq_count = lax.axis_size("seq")
    core_count = lax.axis_size("sub")
    device_count = seq_count * core_count
    token_total = tokens_here * device_count
    heads_here = head_basis_matrix.shape[0]
    head_dim = head_basis_matrix.shape[1]
    rank_dim = head_basis_matrix.shape[2]
    gathered = lax.all_gather(hidden_states, "head", axis=1, tiled=True)
    key_sums = jnp.dot(
        gathered,
        lax.all_gather(key_projection_weight, ("seq", "sub"), axis=0, tiled=True),
        preferred_element_type=jnp.float32,
    )
    value_sums = jnp.dot(
        gathered,
        lax.all_gather(value_projection_weight, ("seq", "sub"), axis=0, tiled=True),
        preferred_element_type=jnp.float32,
    )
    decode_key_cache = key_sums.astype(jnp.bfloat16)
    moments = covariance_sum(decode_key_cache, heads_here, head_dim, token_total)
    value_cache = value_sums.astype(jnp.bfloat16)
    trace_vals = jnp.trace(moments, axis1=1, axis2=2)
    identity = jnp.eye(head_dim, dtype=jnp.float32)
    regular = moments + (ridge_share * trace_vals / head_dim)[:, None, None] * identity
    factor = jnp.linalg.cholesky(regular)
    by_head = jnp.transpose(
        decode_key_cache.astype(jnp.float32).reshape(tokens_here, heads_here, head_dim), (1, 0, 2)
    )
    whitened = lax.linalg.triangular_solve(
        factor, by_head, left_side=False, lower=True, transpose_a=True
    )
    basis_coefficients = jnp.einsum(
        "htd,hdr->htr", whitened, head_basis_matrix, precision=lax.Precision.HIGHEST
    )
    compressed = (
        jnp.transpose(basis_coefficients, (1, 0, 2))
        .reshape(tokens_here, heads_here * rank_dim)
        .astype(jnp.bfloat16)
    )
    row_order = jnp.argsort(slot_token)
    wanted = slot_token[row_order]
    asked = lax.all_to_all(wanted, ("seq", "sub"), split_axis=0, concat_axis=0, tiled=True)
    local_rows = asked % tokens_here
    got_coeffs, got_values = (
        lax.all_to_all(
            compressed[local_rows], ("seq", "sub"), split_axis=0, concat_axis=0, tiled=True
        ),
        lax.all_to_all(
            value_cache[local_rows], ("seq", "sub"), split_axis=0, concat_axis=0, tiled=True
        ),
    )
    inverse = jnp.argsort(row_order)
    return (got_coeffs[inverse], got_values[inverse])


def solution(mesh):
    return jax.shard_map(
        per_device,
        mesh=mesh,
        in_specs=(
            P(("groups", "seq", "sub"), "head"),
            P(("seq", "sub"), "head"),
            P(("seq", "sub"), "head"),
            P("head", None, None),
            P(("groups", "seq", "sub")),
        ),
        out_specs=(P(("groups", "seq", "sub"), "head"), P(("groups", "seq", "sub"), "head")),
        check_vma=False,
    )
```

profile of v0, /device:TPU:0, one launch (start us, length us, event | category | flops | bytes accessed | tf_op | source)
XLA Modules:
  0.0 405.3 jit_solution(3034889648175689121)
XLA Ops:
  7.2 0.0 copy-start
  7.2 0.0 all-gather.4.cloned.1.call-start
  7.2 0.7 all-gather.4.cloned.1.call-update
  7.9 0.0 all-gather.6.cloned.1.call-start
  8.0 0.7 all-gather.6.cloned.1.call-update
  8.7 0.0 copy-start.1
  8.7 0.0 all-reduce.2.cloned.1.call-start
  8.7 107.6 %all-gather.4.cloned.1.call-done = bf16[512,8192]{1,0:T(8,128)(2,1)} async-done(((bf16[512,4096]{1,0:T(8,128)(2,1)}), bf16[512,8192]{1,0:T(8,128)(2,1)}) %all-gather.4.cloned.1.call-update) | async-done | bytes 8388624 | tf_op jit(solution)/shard_map/all_gather | solution.py:29
  116.3 83.7 %all-gather.6.cloned.1.call-done = bf16[8192,512]{1,0:T(8,128)(2,1)} async-done(((bf16[1024,512]{1,0:T(8,128)(2,1)}), bf16[8192,512]{1,0:T(8,128)(2,1)}) %all-gather.6.cloned.1.call-update) | async-done | bytes 8388624 | tf_op jit(solution)/shard_map/all_gather | solution.py:32
  200.0 10.3 %convolution_convert_fusion.1 = bf16[512,512]{0,1:T(8,128)(2,1)S(1)} fusion(bf16[512,8192]{1,0:T(8,128)(2,1)} %all-gather.4.cloned.1.call-done, bf16[8192,512]{1,0:T(8,128)(2,1)} %all-gather.6.cloned.1.call-done), kind=kOutput, calls=%fused_computation.6 | convolution fusion | flops 4295229440 | bytes 17301504 | tf_op jit(solution)/shard_map/dot_general | solution.py:30
  210.3 1.0 fusion.6
  211.3 0.0 all-reduce.2.cloned.1.call-update
  211.3 0.0 all-gather.8.cloned.1.call-start
  211.4 0.5 all-gather.8.cloned.1.call-update
  211.9 0.0 copy-done.1
  211.9 3.8 sort.31
  215.7 3.5 gather_fusion
  219.2 0.7 all_to_all.24
  219.9 3.5 all-to-all-start
  223.4 5.2 %all-to-all-done = s32[8,64,1]{1,2,0:T(1,128)S(1)} async-done(((s32[8,64,1]{1,2,0:T(1,128)}), s32[8,64,1]{1,2,0:T(1,128)S(1)}, u32[]{:S(2)}, u32[]{:S(2)}) %all-to-all-start) | async-done | bytes 2080 | tf_op jit(solution)/shard_map/all_to_all | solution.py:63
  228.6 0.5 broadcast.144
  229.1 0.7 reduce.9
  229.8 0.1 all_to_all.26
  229.9 0.3 copy.19
  230.2 34.9 %all-reduce.2.cloned.1.call-done = f32[4,128,128]{2,1,0:T(8,128)} async-done(((f32[4,128,128]{2,1,0:T(8,128)}), f32[4,128,128]{2,1,0:T(8,128)}) %all-reduce.2.cloned.1.call-update) | async-done | bytes 262160 | tf_op jit(solution)/shard_map/psum | solution.py:14
  265.1 1.1 select_reduce_fusion.1
  266.1 1.0 multiply_add_fusion
  267.2 0.1 copy.21
  267.3 1.1 fusion.3
  268.4 46.9 %custom-call.7 = f32[4,128,128]{2,1,0:T(8,128)S(1)} custom-call(f32[4,128,128]{2,1,0:T(8,128)S(1)} %fusion.3), custom_call_target="Cholesky" | custom-call | tf_op jit(solution)/shard_map/jit(cholesky)/cholesky | solution.py:46
  315.3 0.1 compare_reduce_fusion
  315.5 0.1 select_bitcast_fusion
  315.6 39.3 %custom-call.8 = f32[4,1,128,128]{2,3,1,0:T(8,128)S(1)} custom-call(f32[4,1,128,128]{3,2,1,0:T(8,128)S(1)} %select_bitcast_fusion), custom_call_target="InvertDiagBlocksLowerTriangular" | custom-call | tf_op jit(solution)/shard_map/triangular_solve | solution.py:50
  354.9 0.6 fusion
  355.5 0.0 copy-done
  355.5 1.3 convolution_convert_fusion.2
  356.7 0.1 copy.24
  356.9 2.6 gather_fusion.1
  359.5 3.6 all-to-all-start.1
  363.1 0.0 all-gather.8.cloned.1.call-done
  363.1 10.2 %convolution_convert_fusion = bf16[512,512]{1,0:T(8,128)(2,1)S(1)} fusion(bf16[512,8192]{1,0:T(8,128)(2,1)} %all-gather.4.cloned.1.call-done, bf16[8192,512]{1,0:T(8,128)(2,1)} %all-gather.8.cloned.1.call-done), kind=kOutput, calls=%fused_computation.5 | convolution fusion | flops 4295229440 | bytes 17301504 | tf_op jit(solution)/shard_map/dot_general | solution.py:35
  373.4 2.6 gather_fusion.3
  376.0 0.0 all-to-all-done.1
  376.0 4.8 %all-to-all-start.2 = ((bf16[8,64,512]{2,1,0:T(8,128)(2,1)}), bf16[8,64,512]{2,1,0:T(8,128)(2,1)S(1)}, u32[]{:S(2)}, u32[]{:S(2)}) async-start(bf16[8,64,512]{2,1,0:T(8,128)(2,1)} %bitcast.11), calls=%async_computation.2 | async-start | bytes 1048576 | tf_op jit(solution)/shard_map/all_to_all | solution.py:69
  380.8 3.8 sort.32
  384.6 2.6 gather_fusion.2
  387.2 9.0 %all-to-all-done.2 = bf16[8,64,512]{2,1,0:T(8,128)(2,1)S(1)} async-done(((bf16[8,64,512]{2,1,0:T(8,128)(2,1)}), bf16[8,64,512]{2,1,0:T(8,128)(2,1)S(1)}, u32[]{:S(2)}, u32[]{:S(2)}) %all-to-all-start.2) | async-done | bytes 524320 | tf_op jit(solution)/shard_map/all_to_all | solution.py:69
  396.2 2.6 gather_fusion.4
  (13 shorter events, 0.1 us)
Async XLA Ops:
  7.2 348.3 %copy-start = (f32[4,128,64]{1,2,0:T(8,128)S(1)}, f32[4,128,64]{1,2,0:T(8,128)}, u32[]{:S(2)}) copy-start(f32[4,128,64]{1,2,0:T(8,128)} %param.8) | copy-start | bytes 393220
  7.2 109.1 %all-gather.4.cloned.1.call-start = ((), (), s32[]{:S(2)}) async-start(), calls=%async_computation.3 | async-start | bytes 12582912 | tf_op jit(solution)/shard_map/all_gather | solution.py:29
  7.9 192.1 %all-gather.6.cloned.1.call-start = ((), (), s32[]{:S(2)}) async-start(), calls=%async_computation.4 | async-start | bytes 9437184 | tf_op jit(solution)/shard_map/all_gather | solution.py:32
  8.7 203.2 %copy-start.1 = (s32[512]{0:T(512)S(1)}, s32[512]{0:T(512)}, u32[]{:S(2)}) copy-start(s32[512]{0:T(512)} %param.9) | copy-start | bytes 6148
  8.7 256.4 %all-reduce.2.cloned.1.call-start = ((), (), s32[]{:S(2)}) async-start(), calls=%async_computation.5 | async-start | bytes 524288 | tf_op jit(solution)/shard_map/psum | solution.py:14
  211.3 151.8 %all-gather.8.cloned.1.call-start = ((), (), s32[]{:S(2)}) async-start(), calls=%async_computation.6 | async-start | bytes 9437184 | tf_op jit(solution)/shard_map/all_gather | solution.py:37
  219.9 8.7 %all-to-all-start = ((s32[8,64,1]{1,2,0:T(1,128)}), s32[8,64,1]{1,2,0:T(1,128)S(1)}, u32[]{:S(2)}, u32[]{:S(2)}) async-start(s32[8,64,1]{1,2,0:T(1,128)} %bitcast.7), calls=%async_computation | async-start | bytes 8192 | tf_op jit(solution)/shard_map/all_to_all | solution.py:63
  359.5 16.6 %all-to-all-start.1 = ((bf16[8,64,256]{2,1,0:T(8,128)(2,1)}), bf16[8,64,256]{2,1,0:T(8,128)(2,1)S(1)}, u32[]{:S(2)}, u32[]{:S(2)}) async-start(bf16[8,64,256]{2,1,0:T(8,128)(2,1)} %bitcast.9), calls=%async_computation.1 | async-start | bytes 524288 | tf_op jit(solution)/shard_map/all_to_all | solution.py:66
  376.0 20.1 %all-to-all-start.2 = ((bf16[8,64,512]{2,1,0:T(8,128)(2,1)}), bf16[8,64,512]{2,1,0:T(8,128)(2,1)S(1)}, u32[]{:S(2)}, u32[]{:S(2)}) async-start(bf16[8,64,512]{2,1,0:T(8,128)(2,1)} %bitcast.11), calls=%async_computation.2 | async-start | bytes 1048576 | tf_op jit(solution)/shard_map/all_to_all | solution.py:69
Sparse Core Ops, SparseCore 0:
  9.6 106.6 all-gather.3
  117.9 82.0 all-gather.5
  211.4 53.5 all-reduce.1
  266.6 81.1 all-gather.7
where the time goes:
time: 406 us; the launch traced here: 405 us
  waiting for transfers between devices  242 us (60%)
  other arithmetic  98 us (24%)
  matrix products  23.4 us (6%)
  local copies, waits for them, and re-layouts  15.7 us (4%)
  between operations  13.9 us (3%)
  starting transfers between devices  12.1 us (3%)
    all_gather x1, waiting for transfers between devices, per_device(): gathered = lax.all_gather(hidden_states, 'head', axis=1, tiled=True)  108 us
    all_gather x1, waiting for transfers between devices, per_device(): lax.all_gather(key_projection_weight, ('seq', 'sub'), axis=0, tiled=True)  83.7 us
    another operation x4, other arithmetic, per_device(): factor = jnp.linalg.cholesky(regular)  47.1 us
    another operation x3, other arithmetic, per_device(): lax.linalg.triangular_solve(factor, by_head, left_side=False, lower=True,...  39.4 us
    psum x1, waiting for transfers between devices, covariance_sum(): summed = lax.psum(local_terms, ('seq', 'sub'))  34.9 us
    dot_general x1, matrix products, per_device(): jnp.dot(gathered, lax.all_gather(key_projection_weight, ('seq', 'sub'), a...  10.3 us
    dot_general x1, matrix products, per_device(): jnp.dot(gathered, lax.all_gather(value_projection_weight, ('seq', 'sub'),...  10.2 us
    all_to_all x1, waiting for transfers between devices, per_device(): lax.all_to_all(value_cache[local_rows], ('seq', 'sub'), split_axis=0, con...  9 us
  transfers between devices with their start and end apart: 7, of which 5 were waited for; matrix products, arithmetic and copies ran while one was open for 30% of the time, Pallas kernels for 0%

commit v1 on v0

--- a/solution.py
+++ b/solution.py
@@ -4,6 +4,27 @@
 from jax.sharding import PartitionSpec as P
 
 ridge_share = 0.05
+
+
+def in_order(blocks, dim):
+    dims = list(blocks.shape[1:])
+    dims[dim] *= blocks.shape[0]
+    return jnp.moveaxis(blocks, 0, dim).reshape(dims)
+
+
+def grow_blocks(array, axis):
+    length, position = (lax.axis_size(axis), lax.axis_index(axis))
+    blocks, distance = (array[None], 1)
+    while distance < length:
+        other = lax.ppermute(blocks, axis, [(i, i ^ distance) for i in range(length)])
+        low = position & distance == 0
+        blocks = jnp.concatenate([jnp.where(low, blocks, other), jnp.where(low, other, blocks)])
+        distance *= 2
+    return blocks
+
+
+def doubled_up(value, axis, dim):
+    return in_order(grow_blocks(value, axis), dim)
 
 
 def covariance_sum(decode_key_cache, heads_here, head_dim, token_total):
@@ -29,7 +50,7 @@
     gathered = lax.all_gather(hidden_states, "head", axis=1, tiled=True)
     key_sums = jnp.dot(
         gathered,
-        lax.all_gather(key_projection_weight, ("seq", "sub"), axis=0, tiled=True),
+        doubled_up(key_projection_weight, ("seq", "sub"), 0),
         preferred_element_type=jnp.float32,
     )
     value_sums = jnp.dot(

time: 406 us -> 469 us (1.16)
  waiting for transfers between devices: 242 us -> 280 us
  other arithmetic: 98 us -> 116 us
  starting transfers between devices: 12.1 us -> 19.4 us
    ppermute x0 -> x3, waiting for transfers between devices: none -> 229 us  [grow_blocks(): lax.ppermute(blocks, axis, [(i, i ^ distance) for i in range(length)])]
    all_gather x1, waiting for transfers between devices: 108 us -> 0.01 us  [per_device(): gathered = lax.all_gather(hidden_states, 'head', axis=1, tiled=True)]
    all_gather x1 -> x0, waiting for transfers between devices: 83.7 us -> none  [per_device(): lax.all_gather(key_projection_weight, ('seq', 'sub'), axis=0, tiled=True)]
    concatenate x0 -> x3, other arithmetic: none -> 10.1 us  [grow_blocks(): jnp.concatenate([jnp.where(low, blocks, other), jnp.where(low, other, blo...]
    select_n x0 -> x3, other arithmetic: none -> 7.63 us  [grow_blocks(): jnp.where(low, blocks, other)]
    ppermute x0 -> x3, starting transfers between devices: none -> 6.28 us  [grow_blocks(): lax.ppermute(blocks, axis, [(i, i ^ distance) for i in range(length)])]
  transfers between devices with their start and end apart: 7 -> 9, of which waited for: 5 -> 6; matrix products, arithmetic and copies ran while one was open for 30% -> 30% of each run, Pallas kernels for 0% -> 0%
where the time goes in v1:
time: 469 us
  waiting for transfers between devices  280 us (60%)
  other arithmetic  116 us (25%)
  matrix products  23.4 us (5%)
  starting transfers between devices  19.4 us (4%)
  local copies, waits for them, and re-layouts  16.7 us (4%)
  between operations  14 us (3%)
    ppermute x3, waiting for transfers between devices, grow_blocks(): lax.ppermute(blocks, axis, [(i, i ^ distance) for i in range(length)])  229 us
    another operation x4, other arithmetic, per_device(): factor = jnp.linalg.cholesky(regular)  47.1 us
    another operation x3, other arithmetic, per_device(): lax.linalg.triangular_solve(factor, by_head, left_side=False, lower=True,...  39.4 us
    psum x1, waiting for transfers between devices, covariance_sum(): summed = lax.psum(local_terms, ('seq', 'sub'))  35.7 us
    dot_general x1, matrix products, per_device(): jnp.dot(gathered, doubled_up(key_projection_weight, ('seq', 'sub'), 0), p...  10.3 us
    dot_general x1, matrix products, per_device(): jnp.dot(gathered, lax.all_gather(value_projection_weight, ('seq', 'sub'),...  10.2 us
    concatenate x3, other arithmetic, grow_blocks(): jnp.concatenate([jnp.where(low, blocks, other), jnp.where(low, other, blo...  10.1 us
  transfers between devices with their start and end apart: 9, of which 6 were waited for; matrix products, arithmetic and copies ran while one was open for 30% of the time, Pallas kernels for 0%

profile of v1, /device:TPU:0, one launch (start us, length us, event | category | flops | bytes accessed | tf_op | source)
XLA Modules:
  0.0 469.0 jit_solution(6764524913943199601)
XLA Ops:
  7.2 0.5 collective-permute-start
  7.8 0.2 all-gather.3.cloned.1.call-update
  8.0 2.3 collective-permute-done
  10.3 0.1 broadcast_select_fusion.5
  10.4 1.0 copy-done.3
  11.4 0.2 pad_maximum_fusion.2
  11.6 3.0 collective-permute-start.1
  14.6 46.0 %collective-permute-done.1 = bf16[2,1024,512]{2,1,0:T(8,128)(2,1)} collective-permute-done((bf16[2,1024,512]{2,1,0:T(8,128)(2,1)S(1)}, bf16[2,1024,512]{2,1,0:T(8,128)(2,1)}, u32[]{:S(2)}, u32[]{:S(2)}) %collective-permute-start.1) | collective-permute-done | bytes 2097184 | tf_op jit(solution)/shard_map/ppermute | solution.py:19
  60.6 2.1 broadcast_select_fusion.3
  62.8 2.5 pad_maximum_fusion.1
  65.3 2.8 collective-permute-start.2
  68.1 180.4 %collective-permute-done.2 = bf16[4,1024,512]{2,1,0:T(8,128)(2,1)} collective-permute-done((bf16[4,1024,512]{2,1,0:T(8,128)(2,1)}, bf16[4,1024,512]{2,1,0:T(8,128)(2,1)}, u32[]{:S(2)}, u32[]{:S(2)}) %collective-permute-start.2) | collective-permute-done | bytes 4194336 | tf_op jit(solution)/shard_map/ppermute | solution.py:19
  248.5 5.4 %broadcast_select_fusion.1 = (bf16[4,1024,512]{2,1,0:T(8,128)(2,1)}, bf16[4,1024,512]{2,1,0:T(8,128)(2,1)}) fusion(bf16[4,1024,512]{2,1,0:T(8,128)(2,1)} %collective-permute-done.2, pred[]{:T(512)S(6)} %eq.18, bf16[2,1024,512]{2,1,0:T(8,128)(2,1)} %copy-done.2, bf16[2,1024,512]{2,1,0:T(8,128)(2,1)S(1)} %get-tuple-element.8), kind=kLoop, calls=%fused_computation.8 | loop fusion | flops 6291456 | bytes 16777216 | tf_op jit(solution)/shard_map/jit(_where)/select_n | solution.py:21
  253.9 7.4 %pad_maximum_fusion = bf16[8,1024,512]{2,1,0:T(8,128)(2,1)} fusion(bf16[4,1024,512]{2,1,0:T(8,128)(2,1)} %get-tuple-element.7, bf16[4,1024,512]{2,1,0:T(8,128)(2,1)} %get-tuple-element.6), kind=kLoop, calls=%fused_computation.5 | loop fusion | flops 4194304 | bytes 16777216 | tf_op jit(solution)/shard_map/concatenate | solution.py:21
  261.3 10.3 %convolution_convert_fusion = bf16[512,512]{1,0:T(8,128)(2,1)S(1)} fusion(bf16[8192,512]{1,0:T(8,128)(2,1)} %bitcast.39, bf16[512,8192]{1,0:T(8,128)(2,1)} %all-gather.3.cloned.1.call-done), kind=kOutput, calls=%fused_computation.12 | convolution fusion | flops 4295229440 | bytes 17301504 | tf_op jit(solution)/shard_map/dot_general | solution.py:51
  271.6 1.0 fusion.6
  272.7 0.0 all-gather.5.cloned.1.call-start
  272.7 0.7 all-gather.5.cloned.1.call-update
  273.4 3.8 sort.31
  277.2 3.5 gather_fusion
  280.7 0.7 all_to_all.24
  281.4 4.6 all-to-all-start
  286.0 5.4 %all-to-all-done = s32[8,64,1]{1,2,0:T(1,128)S(1)} async-done(((s32[8,64,1]{1,2,0:T(1,128)}), s32[8,64,1]{1,2,0:T(1,128)S(1)}, u32[]{:S(2)}, u32[]{:S(2)}) %all-to-all-start) | async-done | bytes 2080 | tf_op jit(solution)/shard_map/all_to_all | solution.py:84
  291.5 0.5 broadcast.144
  292.0 0.7 reduce.9
  292.6 0.1 all_to_all.26
  292.7 0.3 copy.19
  293.0 35.7 %all-reduce.2.cloned.1.call-done = f32[4,128,128]{2,1,0:T(8,128)} async-done(((f32[4,128,128]{2,1,0:T(8,128)}), f32[4,128,128]{2,1,0:T(8,128)}) %all-reduce.2.cloned.1.call-update) | async-done | bytes 262160 | tf_op jit(solution)/shard_map/psum | solution.py:35
  328.8 1.1 select_reduce_fusion.1
  329.9 1.0 multiply_add_fusion
  330.9 0.1 copy.21
  331.0 1.1 fusion.3
  332.1 46.9 %custom-call.7 = f32[4,128,128]{2,1,0:T(8,128)S(1)} custom-call(f32[4,128,128]{2,1,0:T(8,128)S(1)} %fusion.3), custom_call_target="Cholesky" | custom-call | tf_op jit(solution)/shard_map/jit(cholesky)/cholesky | solution.py:67
  379.0 0.1 compare_reduce_fusion
  379.2 0.1 select_bitcast_fusion
  379.3 39.3 %custom-call.8 = f32[4,1,128,128]{2,3,1,0:T(8,128)S(1)} custom-call(f32[4,1,128,128]{3,2,1,0:T(8,128)S(1)} %select_bitcast_fusion), custom_call_target="InvertDiagBlocksLowerTriangular" | custom-call | tf_op jit(solution)/shard_map/triangular_solve | solution.py:71
  418.6 0.6 fusion
  419.2 1.3 convolution_convert_fusion.2
  420.4 0.1 copy.24
  420.6 2.6 gather_fusion.1
  423.2 3.6 all-to-all-start.1
  426.8 10.2 %convolution_convert_fusion.1 = bf16[512,512]{1,0:T(8,128)(2,1)S(1)} fusion(bf16[512,8192]{1,0:T(8,128)(2,1)} %all-gather.3.cloned.1.call-done, bf16[8192,512]{1,0:T(8,128)(2,1)} %all-gather.5.cloned.1.call-done), kind=kOutput, calls=%fused_computation.13 | convolution fusion | flops 4295229440 | bytes 17301504 | tf_op jit(solution)/shard_map/dot_general | solution.py:56
  437.1 2.6 gather_fusion.3
  439.7 4.8 %all-to-all-start.2 = ((bf16[8,64,512]{2,1,0:T(8,128)(2,1)}), bf16[8,64,512]{2,1,0:T(8,128)(2,1)S(1)}, u32[]{:S(2)}, u32[]{:S(2)}) async-start(bf16[8,64,512]{2,1,0:T(8,128)(2,1)} %bitcast.15), calls=%async_computation.2 | async-start | bytes 1048576 | tf_op jit(solution)/shard_map/all_to_all | solution.py:90
  444.5 3.8 sort.32
  448.3 2.6 gather_fusion.2
  450.9 9.0 %all-to-all-done.2 = bf16[8,64,512]{2,1,0:T(8,128)(2,1)S(1)} async-done(((bf16[8,64,512]{2,1,0:T(8,128)(2,1)}), bf16[8,64,512]{2,1,0:T(8,128)(2,1)S(1)}, u32[]{:S(2)}, u32[]{:S(2)}) %all-to-all-start.2) | async-done | bytes 524320 | tf_op jit(solution)/shard_map/all_to_all | solution.py:90
  459.9 2.6 gather_fusion.4
  (28 shorter events, 0.3 us)
Async XLA Ops:
  7.2 412.0 %copy-start = (f32[4,128,64]{1,2,0:T(8,128)S(1)}, f32[4,128,64]{1,2,0:T(8,128)}, u32[]{:S(2)}) copy-start(f32[4,128,64]{1,2,0:T(8,128)} %param.8) | copy-start | bytes 393220
  7.2 3.1 copy-start.4
  7.2 254.1 %all-gather.3.cloned.1.call-start = ((), (), s32[]{:S(2)}) async-start(), calls=%async_computation.3 | async-start | bytes 12582912 | tf_op jit(solution)/shard_map/all_gather | solution.py:50
  7.2 3.0 collective-permute-start
  7.9 320.8 %all-reduce.2.cloned.1.call-start = ((), (), s32[]{:S(2)}) async-start(), calls=%async_computation.4 | async-start | bytes 524288 | tf_op jit(solution)/shard_map/psum | solution.py:35
  10.4 1.0 copy-start.3
  11.6 49.0 %collective-permute-start.1 = (bf16[2,1024,512]{2,1,0:T(8,128)(2,1)S(1)}, bf16[2,1024,512]{2,1,0:T(8,128)(2,1)}, u32[]{:S(2)}, u32[]{:S(2)}) collective-permute-start(bf16[2,1024,512]{2,1,0:T(8,128)(2,1)S(1)} %pad_maximum_fusion.2), channel_id=1, source_target_pairs={{0,4},{1,5},{4,0},{5,1},{8,12},{9,13},{12,8},{13,9},{2,6},{3,7},{6... | collective-permute-start | bytes 6291464 | tf_op jit(solution)/shard_map/ppermute | solution.py:19
  62.8 2.6 copy-start.2
  65.3 183.2 %collective-permute-start.2 = (bf16[4,1024,512]{2,1,0:T(8,128)(2,1)}, bf16[4,1024,512]{2,1,0:T(8,128)(2,1)}, u32[]{:S(2)}, u32[]{:S(2)}) collective-permute-start(bf16[4,1024,512]{2,1,0:T(8,128)(2,1)} %pad_maximum_fusion.1), channel_id=1, source_target_pairs={{0,8},{1,9},{4,12},{5,13},{8,0},{9,1},{12,4},{13,5},{2,10},{3,11},... | collective-permute-start | bytes 12582920 | tf_op jit(solution)/shard_map/ppermute | solution.py:19
  261.3 12.1 %copy-start.1 = (s32[512]{0:T(512)S(1)}, s32[512]{0:T(512)}, u32[]{:S(2)}) copy-start(s32[512]{0:T(512)} %param.9) | copy-start | bytes 6148
  272.7 154.2 %all-gather.5.cloned.1.call-start = ((), (), s32[]{:S(2)}) async-start(), calls=%async_computation.5 | async-start | bytes 9437184 | tf_op jit(solution)/shard_map/all_gather | solution.py:58
  281.4 10.1 %all-to-all-start = ((s32[8,64,1]{1,2,0:T(1,128)}), s32[8,64,1]{1,2,0:T(1,128)S(1)}, u32[]{:S(2)}, u32[]{:S(2)}) async-start(s32[8,64,1]{1,2,0:T(1,128)} %bitcast.11), calls=%async_computation | async-start | bytes 8192 | tf_op jit(solution)/shard_map/all_to_all | solution.py:84
  423.2 16.6 %all-to-all-start.1 = ((bf16[8,64,256]{2,1,0:T(8,128)(2,1)}), bf16[8,64,256]{2,1,0:T(8,128)(2,1)S(1)}, u32[]{:S(2)}, u32[]{:S(2)}) async-start(bf16[8,64,256]{2,1,0:T(8,128)(2,1)} %bitcast.13), calls=%async_computation.1 | async-start | bytes 524288 | tf_op jit(solution)/shard_map/all_to_all | solution.py:87
  439.7 20.1 %all-to-all-start.2 = ((bf16[8,64,512]{2,1,0:T(8,128)(2,1)}), bf16[8,64,512]{2,1,0:T(8,128)(2,1)S(1)}, u32[]{:S(2)}, u32[]{:S(2)}) async-start(bf16[8,64,512]{2,1,0:T(8,128)(2,1)} %bitcast.15), calls=%async_computation.2 | async-start | bytes 1048576 | tf_op jit(solution)/shard_map/all_to_all | solution.py:90
Sparse Core Ops, SparseCore 0:
  9.6 106.6 all-gather.2
  272.8 55.9 all-reduce.1
  330.5 81.1 all-gather.4
